TPU v7x, 32 devices: a whole 2x2x4 slice. The times are simulated.
32 devices in a mesh: parts: 2 (over y), pol: 4 (over z), scen: 2 (over x), fund: 2 (over core).
Axes of the slice: x: 2, y: 2, z: 4, core: 2. Of those that a mesh axis runs over, the one named last changes fastest.
Arguments:
- count_init: float32 [32768], P(('pol', 'fund')), may hold values from 0.5 to 2
- value_init: float32 [32768], P(('pol', 'fund')), may hold values from 0.5 to 4
- durations: int32 [32768], P(('pol', 'fund')), may hold values from 0 to 119
- products: int32 [32768], P(('pol', 'fund')), may hold values from 0 to 7
- policy_fund: int32 [32768], P(('pol', 'fund')), may hold values from 0 to 119, as said below
- lapse_base: float32 [8], replicated, may hold values from 0.05 to 0.1
- lapse_sens: float32 [8], replicated, may hold values from 6 to 10
- fee_rate: float32 [8], replicated, may hold values from 0.002 to 0.02
- fund_share: float32 [120], replicated, may hold values from 0.3 to 1
- bond_flows: float32 [16384, 120], P(('pol', 'fund')), may hold values from 0.05 to 1
- bond_fund: int32 [16384], P(('pol', 'fund')), may hold values from 0 to 119, as said below
- holdings: float32 [16384], P(('pol', 'fund')), may hold values from 0.037 to 0.3
- scen_rates: float32 [3, 120, 512], P(None, None, ('parts', 'scen')), parts along dimension 2, may hold values from 0 to 0.12
Outputs:
- credited: float32 [3, 120, 512], P(None, None, ('parts', 'scen')), parts along dimension 2
- reserve: float32 [512, 32768], P(('parts', 'scen'), ('pol', 'fund')), parts along dimension 0
There are 2 independent parts, one for each index of `parts`. A program takes and returns all parts, laid end to end along the dimension named above; an argument that names none is the same for every part. Nothing has to cross between parts.
Inputs may be any that keep to these rules, and one draw needn't show every extreme that they name: `policy_fund`: every fund number appears at least once. `bond_fund`: every fund number appears at least once.
All inputs are finite; a program needn't handle non-finite values.
Results may differ from a plain program's by a relative error of at most 0.0003.
Values sent between devices are 32-bit elements; how exact they have to be, the bound alone decides.
A program may use at most 64 MiB of HBM per device.

v0:
```python
import math

import jax
import jax.numpy as jnp
from jax import lax
from jax.sharding import PartitionSpec as P

surrender_end = 84
highest = lax.Precision.HIGHEST
contract_cols = (((1,), (1,)), ((), ()))
contract_rows = (((0,), (0,)), ((), ()))


def onehot_cols(fund_ids, offset_at, breadth, fund_count):
    picked = lax.dynamic_slice_in_dim(fund_ids, offset_at, breadth, 0)
    return (lax.broadcasted_iota(jnp.int32, (fund_count, breadth), 0) == picked[None, :]).astype(
        jnp.float32
    )


def lookup(code_ids, values):
    kind_count = values.shape[0]
    matches = (
        lax.broadcasted_iota(jnp.int32, (kind_count, code_ids.shape[0]), 0) == code_ids[None, :]
    )
    return jnp.sum(jnp.where(matches, values[:, None], 0.0), axis=0)


def fund_totals(weights, fund_ids, fund_count, breadth):
    scen_rows, pol_count = weights.shape

    def add_block(block_idx, running):
        offset_at = block_idx * breadth
        onehot = onehot_cols(fund_ids, offset_at, breadth, fund_count)
        piece_blk = lax.dynamic_slice_in_dim(weights, offset_at, breadth, 1)
        return running + lax.dot_general(
            onehot, piece_blk, contract_cols, precision=highest, preferred_element_type=jnp.float32
        )

    return lax.fori_loop(
        0, pol_count // breadth, add_block, jnp.zeros((fund_count, scen_rows), jnp.float32)
    )


def advance(
    in_force,
    account,
    credited,
    market,
    lapse_pol,
    sens_pol,
    fee_pol,
    durations,
    fund_ids,
    month_idx,
    breadth,
    want_totals,
):
    fund_count = credited.shape[0]
    scen_rows, pol_count = in_force.shape

    def move_block(block_idx, carried):
        force_all, account_all, running = carried
        offset_at = block_idx * breadth
        onehot = onehot_cols(fund_ids, offset_at, breadth, fund_count)
        credit_pol = lax.dot_general(
            credited, onehot, contract_rows, precision=highest, preferred_element_type=jnp.float32
        )
        force_blk = lax.dynamic_slice_in_dim(force_all, offset_at, breadth, 1)
        account_blk = lax.dynamic_slice_in_dim(account_all, offset_at, breadth, 1)
        lapse_blk = lax.dynamic_slice_in_dim(lapse_pol, offset_at, breadth, 0)
        sens_blk = lax.dynamic_slice_in_dim(sens_pol, offset_at, breadth, 0)
        fee_blk = lax.dynamic_slice_in_dim(fee_pol, offset_at, breadth, 0)
        dur_blk = lax.dynamic_slice_in_dim(durations, offset_at, breadth, 0)
        later_mult = jnp.where(dur_blk + month_idx >= surrender_end, 2.0, 1.0)
        lapse_now = (lapse_blk * later_mult)[None, :] * jnp.exp(
            sens_blk[None, :] * (market[:, None] - credit_pol)
        )
        force_new = force_blk * jnp.exp(-lapse_now)
        account_new = account_blk * jnp.exp(credit_pol / 12.0 - fee_blk[None, :])
        force_all = lax.dynamic_update_slice_in_dim(force_all, force_new, offset_at, 1)
        account_all = lax.dynamic_update_slice_in_dim(account_all, account_new, offset_at, 1)
        if want_totals:
            running = running + lax.dot_general(
                onehot,
                force_new * account_new,
                contract_cols,
                precision=highest,
                preferred_element_type=jnp.float32,
            )
        return (force_all, account_all, running)

    return lax.fori_loop(
        0,
        pol_count // breadth,
        move_block,
        (in_force, account, jnp.zeros((fund_count, scen_rows), jnp.float32)),
    )


def local(
    count_init,
    value_init,
    durations,
    products,
    policy_fund,
    lapse_base,
    lapse_sens,
    fee_rate,
    fund_share,
    bond_flows,
    bond_fund,
    holdings,
    scen_rates,
):
    fund_count = fund_share.shape[0]
    months = scen_rates.shape[0]
    tenors = scen_rates.shape[1]
    scen_rows = scen_rates.shape[2]
    pol_count = count_init.shape[0]
    breadth = math.gcd(pol_count, 1024)
    tenor_years = (jnp.arange(tenors).astype(jnp.float32) + 1.0) / 12.0
    lapse_pol = lookup(products, lapse_base)
    sens_pol = lookup(products, lapse_sens)
    fee_pol = lookup(products, fee_rate)
    bond_onehot = onehot_cols(bond_fund, 0, bond_fund.shape[0], fund_count)

    def asset_part(month_num):
        discount = jnp.exp(-scen_rates[month_num] * tenor_years[:, None])
        bond_values = jnp.dot(
            bond_flows, discount, precision=highest, preferred_element_type=jnp.float32
        )
        return jnp.dot(
            bond_onehot,
            bond_values * holdings[:, None],
            precision=highest,
            preferred_element_type=jnp.float32,
        )

    asset_stack = lax.psum(
        jnp.stack([asset_part(month_num) for month_num in range(months)]), ("pol", "fund")
    )
    start_totals = fund_totals((count_init * value_init)[None, :], policy_fund, fund_count, breadth)
    liab_part = jnp.broadcast_to(start_totals, (fund_count, scen_rows))
    in_force = jnp.broadcast_to(count_init[None, :], (scen_rows, pol_count))
    account = jnp.broadcast_to(value_init[None, :], (scen_rows, pol_count))
    credited_list = []
    for month_idx in range(months):
        assets = asset_stack[month_idx]
        liabilities = lax.psum(liab_part, ("pol", "fund"))
        credited = fund_share[:, None] * jnp.log(assets / liabilities)
        market = scen_rates[month_idx, tenors - 1]
        in_force, account, liab_part = advance(
            in_force,
            account,
            credited,
            market,
            lapse_pol,
            sens_pol,
            fee_pol,
            durations,
            policy_fund,
            month_idx,
            breadth,
            month_idx < months - 1,
        )
        credited_list.append(credited)
    return (jnp.stack(credited_list), in_force * account)


def solution(mesh):
    in_specs = (
        P(("pol", "fund")),
        P(("pol", "fund")),
        P(("pol", "fund")),
        P(("pol", "fund")),
        P(("pol", "fund")),
        P(),
        P(),
        P(),
        P(),
        P(("pol", "fund"), None),
        P(("pol", "fund")),
        P(("pol", "fund")),
        P(None, None, ("parts", "scen")),
    )
    out_specs = (P(None, None, ("parts", "scen")), P(("parts", "scen"), ("pol", "fund")))
    return jax.shard_map(local, mesh=mesh, in_specs=in_specs, out_specs=out_specs, check_vma=False)
```

profile of v0, /device:TPU:0, one launch (start us, length us, event | category | flops | bytes accessed | tf_op | source)
XLA Modules:
  0.0 272.6 jit_solution(3409827075269828922)
XLA Ops:
  8.4 1.9 convolution_multiply_fusion
  17.2 30.9 %psum.29 = f32[120,128]{1,0:T(8,128)S(1)} all-reduce(f32[120,128]{1,0:T(8,128)S(1)} %broadcast_in_dim.151), channel_id=1, replica_groups=mesh['parts'=2,'pol'=4,'scen'=2,'fund'=2] {'pol','fund'}, use_global_device_ids=true, to_apply=%region_3.4 | all-reduce | flops 15360 | bytes 122880 | tf_op jit(solution)/shard_map/psum | solution.py:150
  48.3 24.1 %all-reduce.2.cloned.1.call-done = f32[3,120,128]{2,1,0:T(8,128)} async-done(((f32[3,120,128]{2,1,0:T(8,128)}), f32[3,120,128]{2,1,0:T(8,128)}) %all-reduce.2.cloned.1.call-update) | async-done | bytes 184336 | tf_op jit(solution)/shard_map/psum | solution.py:140
  74.0 1.9 broadcast_in_dim.153
  75.9 57.0 %while.67 = (s32[]{:T(128)}, f32[128,4096]{0,1:T(8,128)S(1)}, f32[128,4096]{0,1:T(8,128)}, f32[120,128]{1,0:T(8,128)S(1)}, f32[4096]{0:T(1024)S(1)}, /*index=5*/...) while((s32[]{:T(128)}, f32[128,4096]{0,1:T(8,128)S(1)}, ...), condition=%wide.region_8.9_spmd.clone, body=%wide.region_7.8_spmd.clone.sunk | while | flops 379995136 | bytes 21226716 | solution.py:93
  76.0 3.1 %copy.21 = f32[128,4096]{0,1:T(8,128)} copy(f32[128,4096]{0,1:T(8,128)} %get-tuple-element.1082) | data formatting | bytes 4194304 | tf_op jit(solution)/shard_map/while
  80.3 3.1 %constant_dynamic-update-slice_fusion.6 = (f32[128,4096]{0,1:T(8,128)}, f32[128,4096]{0,1:T(8,128)}, f32[1024,128]{1,0:T(8,128)}) fusion(f32[128,4096]{0,1:T(8,128)} %copy.21, s32[]{:T(128)S(6)} %select_n.110, f32[1024]{0:T(1024)S(1)} %dynamic_slice.256, f32[128,4096]{0,1:T(8,128)} %copy.22, f32[128]{0:T(128)S(1)} %bitcast.142, ...), kind=kOutput, calls=%fused_computation.27.clone.1 | convolution fusion | flops 189915136 | bytes 2699780 | tf_op jit(solution)/shard_map/while/body/eval_jaxpr/dot_general | solution.py:66
  83.5 2.0 convolution_add_fusion.4
  87.1 3.0 %copy.42 = f32[128,4096]{0,1:T(8,128)} copy(f32[128,4096]{0,1:T(8,128)} %get-tuple-element.1097) | data formatting | bytes 4194304 | tf_op jit(solution)/shard_map/while
  90.2 3.1 %copy.21 = f32[128,4096]{0,1:T(8,128)} copy(f32[128,4096]{0,1:T(8,128)} %get-tuple-element.1082) | data formatting | bytes 4194304 | tf_op jit(solution)/shard_map/while
  94.6 3.2 %constant_dynamic-update-slice_fusion.6 = (f32[128,4096]{0,1:T(8,128)}, f32[128,4096]{0,1:T(8,128)}, f32[1024,128]{1,0:T(8,128)}) fusion(f32[128,4096]{0,1:T(8,128)} %copy.21, s32[]{:T(128)S(6)} %select_n.110, f32[1024]{0:T(1024)S(1)} %dynamic_slice.256, f32[128,4096]{0,1:T(8,128)} %copy.22, f32[128]{0:T(128)S(1)} %bitcast.142, ...), kind=kOutput, calls=%fused_computation.27.clone.1 | convolution fusion | flops 189915136 | bytes 2699780 | tf_op jit(solution)/shard_map/while/body/eval_jaxpr/dot_general | solution.py:66
  97.7 2.0 convolution_add_fusion.4
  101.3 3.0 %copy.42 = f32[128,4096]{0,1:T(8,128)} copy(f32[128,4096]{0,1:T(8,128)} %get-tuple-element.1097) | data formatting | bytes 4194304 | tf_op jit(solution)/shard_map/while
  104.4 3.1 %copy.21 = f32[128,4096]{0,1:T(8,128)} copy(f32[128,4096]{0,1:T(8,128)} %get-tuple-element.1082) | data formatting | bytes 4194304 | tf_op jit(solution)/shard_map/while
  108.8 3.2 %constant_dynamic-update-slice_fusion.6 = (f32[128,4096]{0,1:T(8,128)}, f32[128,4096]{0,1:T(8,128)}, f32[1024,128]{1,0:T(8,128)}) fusion(f32[128,4096]{0,1:T(8,128)} %copy.21, s32[]{:T(128)S(6)} %select_n.110, f32[1024]{0:T(1024)S(1)} %dynamic_slice.256, f32[128,4096]{0,1:T(8,128)} %copy.22, f32[128]{0:T(128)S(1)} %bitcast.142, ...), kind=kOutput, calls=%fused_computation.27.clone.1 | convolution fusion | flops 189915136 | bytes 2699780 | tf_op jit(solution)/shard_map/while/body/eval_jaxpr/dot_general | solution.py:66
  112.0 2.0 convolution_add_fusion.4
  115.6 3.0 %copy.42 = f32[128,4096]{0,1:T(8,128)} copy(f32[128,4096]{0,1:T(8,128)} %get-tuple-element.1097) | data formatting | bytes 4194304 | tf_op jit(solution)/shard_map/while
  118.7 3.1 %copy.21 = f32[128,4096]{0,1:T(8,128)} copy(f32[128,4096]{0,1:T(8,128)} %get-tuple-element.1082) | data formatting | bytes 4194304 | tf_op jit(solution)/shard_map/while
  123.1 3.2 %constant_dynamic-update-slice_fusion.6 = (f32[128,4096]{0,1:T(8,128)}, f32[128,4096]{0,1:T(8,128)}, f32[1024,128]{1,0:T(8,128)}) fusion(f32[128,4096]{0,1:T(8,128)} %copy.21, s32[]{:T(128)S(6)} %select_n.110, f32[1024]{0:T(1024)S(1)} %dynamic_slice.256, f32[128,4096]{0,1:T(8,128)} %copy.22, f32[128]{0:T(128)S(1)} %bitcast.142, ...), kind=kOutput, calls=%fused_computation.27.clone.1 | convolution fusion | flops 189915136 | bytes 2699780 | tf_op jit(solution)/shard_map/while/body/eval_jaxpr/dot_general | solution.py:66
  126.2 2.0 convolution_add_fusion.4
  129.8 3.0 %copy.42 = f32[128,4096]{0,1:T(8,128)} copy(f32[128,4096]{0,1:T(8,128)} %get-tuple-element.1097) | data formatting | bytes 4194304 | tf_op jit(solution)/shard_map/while
  132.9 27.7 %psum.30 = f32[120,128]{1,0:T(8,128)S(1)} all-reduce(f32[120,128]{1,0:T(8,128)S(1)} %get-tuple-element.624), channel_id=1, replica_groups=mesh['parts'=2,'pol'=4,'scen'=2,'fund'=2] {'pol','fund'}, use_global_device_ids=true, to_apply=%region_9.10 | all-reduce | flops 15360 | bytes 122880 | tf_op jit(solution)/shard_map/psum | solution.py:150
  161.6 57.0 %while.68 = (s32[]{:T(128)}, f32[128,4096]{0,1:T(8,128)S(1)}, f32[128,4096]{0,1:T(8,128)}, f32[120,128]{1,0:T(8,128)S(1)}, f32[4096]{0:T(1024)S(1)}, /*index=5*/...) while((s32[]{:T(128)}, f32[128,4096]{0,1:T(8,128)S(1)}, ...), condition=%wide.region_11.12_spmd.clone, body=%wide.region_10.11_spmd.clone.sunk | while | flops 379996160 | bytes 21226716 | solution.py:93
  161.6 3.1 %copy.23 = f32[128,4096]{0,1:T(8,128)} copy(f32[128,4096]{0,1:T(8,128)} %get-tuple-element.1127) | data formatting | bytes 4194304 | tf_op jit(solution)/shard_map/while
  166.0 3.1 %constant_dynamic-update-slice_fusion.7 = (f32[128,4096]{0,1:T(8,128)}, f32[128,4096]{0,1:T(8,128)}, f32[1024,128]{1,0:T(8,128)}) fusion(f32[128,4096]{0,1:T(8,128)} %copy.23, s32[]{:T(128)S(6)} %select_n.112, f32[1024]{0:T(1024)S(1)} %dynamic_slice.264, f32[128,4096]{0,1:T(8,128)} %copy.24, f32[128]{0:T(128)S(1)} %bitcast.140, ...), kind=kOutput, calls=%fused_computation.39.clone.1 | convolution fusion | flops 189915136 | bytes 2699780 | tf_op jit(solution)/shard_map/while/body/eval_jaxpr/dot_general | solution.py:66
  169.2 2.0 convolution_add_fusion.5
  172.8 3.0 %copy.54 = f32[128,4096]{0,1:T(8,128)} copy(f32[128,4096]{0,1:T(8,128)} %get-tuple-element.1142) | data formatting | bytes 4194304 | tf_op jit(solution)/shard_map/while
  175.9 3.1 %copy.23 = f32[128,4096]{0,1:T(8,128)} copy(f32[128,4096]{0,1:T(8,128)} %get-tuple-element.1127) | data formatting | bytes 4194304 | tf_op jit(solution)/shard_map/while
  180.2 3.2 %constant_dynamic-update-slice_fusion.7 = (f32[128,4096]{0,1:T(8,128)}, f32[128,4096]{0,1:T(8,128)}, f32[1024,128]{1,0:T(8,128)}) fusion(f32[128,4096]{0,1:T(8,128)} %copy.23, s32[]{:T(128)S(6)} %select_n.112, f32[1024]{0:T(1024)S(1)} %dynamic_slice.264, f32[128,4096]{0,1:T(8,128)} %copy.24, f32[128]{0:T(128)S(1)} %bitcast.140, ...), kind=kOutput, calls=%fused_computation.39.clone.1 | convolution fusion | flops 189915136 | bytes 2699780 | tf_op jit(solution)/shard_map/while/body/eval_jaxpr/dot_general | solution.py:66
  183.4 2.0 convolution_add_fusion.5
  187.0 3.0 %copy.54 = f32[128,4096]{0,1:T(8,128)} copy(f32[128,4096]{0,1:T(8,128)} %get-tuple-element.1142) | data formatting | bytes 4194304 | tf_op jit(solution)/shard_map/while
  190.1 3.1 %copy.23 = f32[128,4096]{0,1:T(8,128)} copy(f32[128,4096]{0,1:T(8,128)} %get-tuple-element.1127) | data formatting | bytes 4194304 | tf_op jit(solution)/shard_map/while
  194.5 3.2 %constant_dynamic-update-slice_fusion.7 = (f32[128,4096]{0,1:T(8,128)}, f32[128,4096]{0,1:T(8,128)}, f32[1024,128]{1,0:T(8,128)}) fusion(f32[128,4096]{0,1:T(8,128)} %copy.23, s32[]{:T(128)S(6)} %select_n.112, f32[1024]{0:T(1024)S(1)} %dynamic_slice.264, f32[128,4096]{0,1:T(8,128)} %copy.24, f32[128]{0:T(128)S(1)} %bitcast.140, ...), kind=kOutput, calls=%fused_computation.39.clone.1 | convolution fusion | flops 189915136 | bytes 2699780 | tf_op jit(solution)/shard_map/while/body/eval_jaxpr/dot_general | solution.py:66
  197.7 2.0 convolution_add_fusion.5
  201.3 3.0 %copy.54 = f32[128,4096]{0,1:T(8,128)} copy(f32[128,4096]{0,1:T(8,128)} %get-tuple-element.1142) | data formatting | bytes 4194304 | tf_op jit(solution)/shard_map/while
  204.3 3.1 %copy.23 = f32[128,4096]{0,1:T(8,128)} copy(f32[128,4096]{0,1:T(8,128)} %get-tuple-element.1127) | data formatting | bytes 4194304 | tf_op jit(solution)/shard_map/while
  208.7 3.2 %constant_dynamic-update-slice_fusion.7 = (f32[128,4096]{0,1:T(8,128)}, f32[128,4096]{0,1:T(8,128)}, f32[1024,128]{1,0:T(8,128)}) fusion(f32[128,4096]{0,1:T(8,128)} %copy.23, s32[]{:T(128)S(6)} %select_n.112, f32[1024]{0:T(1024)S(1)} %dynamic_slice.264, f32[128,4096]{0,1:T(8,128)} %copy.24, f32[128]{0:T(128)S(1)} %bitcast.140, ...), kind=kOutput, calls=%fused_computation.39.clone.1 | convolution fusion | flops 189915136 | bytes 2699780 | tf_op jit(solution)/shard_map/while/body/eval_jaxpr/dot_general | solution.py:66
  211.9 2.0 convolution_add_fusion.5
  215.5 3.0 %copy.54 = f32[128,4096]{0,1:T(8,128)} copy(f32[128,4096]{0,1:T(8,128)} %get-tuple-element.1142) | data formatting | bytes 4194304 | tf_op jit(solution)/shard_map/while
  218.6 26.4 %psum.31 = f32[120,128]{1,0:T(8,128)S(1)} all-reduce(f32[120,128]{1,0:T(8,128)S(1)} %get-tuple-element.627), channel_id=1, replica_groups=mesh['parts'=2,'pol'=4,'scen'=2,'fund'=2] {'pol','fund'}, use_global_device_ids=true, to_apply=%region_12.13 | all-reduce | flops 15360 | bytes 122880 | tf_op jit(solution)/shard_map/psum | solution.py:150
  245.8 11.2 %while.65 = (s32[]{:T(128)}, f32[128,4096]{0,1:T(8,128)S(1)}, f32[128,4096]{0,1:T(8,128)}, f32[4096]{0:T(1024)S(1)}, s32[4096]{0:T(1024)S(1)}, /*index=5*/f32[40...) while((s32[]{:T(128)}, f32[128,4096]{0,1:T(8,128)S(1)}, ...), condition=%wide.region_14.15_spmd, body=%wide.region_13.14_spmd.sunk | while | flops 189919232 | bytes 2212551 | solution.py:93
  245.9 2.8 %fusion.63 = (f32[128,4096]{0,1:T(8,128)}, f32[128,4096]{0,1:T(8,128)S(1)}) fusion(f32[128,4096]{0,1:T(8,128)} %get-tuple-element.1171, s32[]{:T(128)S(6)} %select_n.107, f32[1024]{0:T(1024)S(1)} %dynamic_slice.246, f32[128,4096]{0,1:T(8,128)S(1)} %get-tuple-element.1170, f32[128]{0:T(128)S(1)} %bitcast.144, f32[1024]{0:T(1024)S(1)} %dynamic_slice.247, ...), kind=kOutput, calls=%fused_computation.1.clone.1 | convolution fusion | flops 189915136 | bytes 2175492 | tf_op jit(solution)/shard_map/while/body/eval_jaxpr/dot_general | solution.py:66
  248.7 2.8 %fusion.63 = (f32[128,4096]{0,1:T(8,128)}, f32[128,4096]{0,1:T(8,128)S(1)}) fusion(f32[128,4096]{0,1:T(8,128)} %get-tuple-element.1171, s32[]{:T(128)S(6)} %select_n.107, f32[1024]{0:T(1024)S(1)} %dynamic_slice.246, f32[128,4096]{0,1:T(8,128)S(1)} %get-tuple-element.1170, f32[128]{0:T(128)S(1)} %bitcast.144, f32[1024]{0:T(1024)S(1)} %dynamic_slice.247, ...), kind=kOutput, calls=%fused_computation.1.clone.1 | convolution fusion | flops 189915136 | bytes 2175492 | tf_op jit(solution)/shard_map/while/body/eval_jaxpr/dot_general | solution.py:66
  251.5 2.8 %fusion.63 = (f32[128,4096]{0,1:T(8,128)}, f32[128,4096]{0,1:T(8,128)S(1)}) fusion(f32[128,4096]{0,1:T(8,128)} %get-tuple-element.1171, s32[]{:T(128)S(6)} %select_n.107, f32[1024]{0:T(1024)S(1)} %dynamic_slice.246, f32[128,4096]{0,1:T(8,128)S(1)} %get-tuple-element.1170, f32[128]{0:T(128)S(1)} %bitcast.144, f32[1024]{0:T(1024)S(1)} %dynamic_slice.247, ...), kind=kOutput, calls=%fused_computation.1.clone.1 | convolution fusion | flops 189915136 | bytes 2175492 | tf_op jit(solution)/shard_map/while/body/eval_jaxpr/dot_general | solution.py:66
  254.3 2.8 %fusion.63 = (f32[128,4096]{0,1:T(8,128)}, f32[128,4096]{0,1:T(8,128)S(1)}) fusion(f32[128,4096]{0,1:T(8,128)} %get-tuple-element.1171, s32[]{:T(128)S(6)} %select_n.107, f32[1024]{0:T(1024)S(1)} %dynamic_slice.246, f32[128,4096]{0,1:T(8,128)S(1)} %get-tuple-element.1170, f32[128]{0:T(128)S(1)} %bitcast.144, f32[1024]{0:T(1024)S(1)} %dynamic_slice.247, ...), kind=kOutput, calls=%fused_computation.1.clone.1 | convolution fusion | flops 189915136 | bytes 2175492 | tf_op jit(solution)/shard_map/while/body/eval_jaxpr/dot_general | solution.py:66
  257.1 1.8 copy.17
  258.9 3.0 %copy.18 = f32[128,4096]{1,0:T(8,128)} copy(f32[128,4096]{0,1:T(8,128)} %get-tuple-element.631) | data formatting | bytes 4194304 | tf_op jit(solution)/shard_map/while | solution.py:93
  261.9 3.1 %mul.323 = f32[128,4096]{1,0:T(8,128)} multiply(f32[128,4096]{1,0:T(8,128)S(1)} %copy-done.1, f32[128,4096]{1,0:T(8,128)} %copy.18) | non-fusion elementwise | flops 524288 | bytes 6291456 | tf_op jit(solution)/shard_map/mul | solution.py:168
  (122 shorter events, 36.7 us)
Async XLA Ops:
  7.2 1.2 copy-start
  7.2 3.1 %copy-start.5 = (f32[2048]{0:T(1024)S(1)}, f32[2048]{0:T(1024)}, u32[]{:S(2)}) copy-start(f32[2048]{0:T(1024)} %param.32) | copy-start | bytes 24580
  7.2 3.1 %copy-start.4 = (f32[3,120,128]{2,1,0:T(8,128)S(1)}, f32[3,120,128]{2,1,0:T(8,128)}, u32[]{:S(2)}) copy-start(f32[3,120,128]{2,1,0:T(8,128)} %param.33) | copy-start | bytes 552964
  7.2 65.3 %all-reduce.2.cloned.1.call-start = ((), (), s32[]{:S(2)}) async-start(), calls=%async_computation | async-start | bytes 368640 | tf_op jit(solution)/shard_map/psum | solution.py:140
  10.3 2.2 copy-start.6
  12.6 3.1 %copy-start.7 = (f32[4096]{0:T(1024)S(1)}, f32[4096]{0:T(1024)}, u32[]{:S(2)}) copy-start(f32[4096]{0:T(1024)} %param.21) | copy-start | bytes 49156
  12.6 3.1 %copy-start.8 = (f32[4096]{0:T(1024)S(1)}, f32[4096]{0:T(1024)}, u32[]{:S(2)}) copy-start(f32[4096]{0:T(1024)} %param.22) | copy-start | bytes 49156
  12.6 3.1 %copy-start.2 = (s32[4096]{0:T(1024)S(1)}, s32[4096]{0:T(1024)}, u32[]{:S(2)}) copy-start(s32[4096]{0:T(1024)} %param.25) | copy-start | bytes 49156
  13.4 34.8 %copy-start.9 = (s32[4096]{0:T(1024)S(1)}, s32[4096]{0:T(1024)}, u32[]{:S(2)}) copy-start(s32[4096]{0:T(1024)} %param.24) | copy-start | bytes 49156
  13.4 34.7 %copy-start.11 = (f32[8]{0:T(128)S(1)}, f32[8]{0:T(128)}, u32[]{:S(2)}) copy-start(f32[8]{0:T(128)} %param.28) | copy-start | bytes 100
  13.4 34.7 %copy-start.12 = (f32[8]{0:T(128)S(1)}, f32[8]{0:T(128)}, u32[]{:S(2)}) copy-start(f32[8]{0:T(128)} %param.27) | copy-start | bytes 100
  13.4 34.7 %copy-start.13 = (f32[8]{0:T(128)S(1)}, f32[8]{0:T(128)}, u32[]{:S(2)}) copy-start(f32[8]{0:T(128)} %param.26) | copy-start | bytes 100
  13.4 59.0 %copy-start.10 = (f32[120]{0:T(128)S(1)}, f32[120]{0:T(128)}, u32[]{:S(2)}) copy-start(f32[120]{0:T(128)} %param.29) | copy-start | bytes 1444
  73.4 2.5 copy-start.3
  258.9 3.0 %copy-start.1 = (f32[128,4096]{1,0:T(8,128)S(1)}, f32[128,4096]{1,0:T(8,128)}, u32[]{:S(2)}) copy-start(f32[128,4096]{1,0:T(8,128)} %copy.17) | copy-start | bytes 6291460
Sparse Core Ops, SparseCore 0:
  15.8 56.6 all-reduce.1
where the time goes:
time: 274 us; the launch traced here: 273 us
  blocking collectives  85 us (31%)
  local copies, waits for them, and re-layouts  81 us (30%)
  matrix products  60 us (22%)
  waiting for transfers between devices  24.1 us (9%)
  between operations  14.4 us (5%)
  other arithmetic  7.53 us (3%)
    psum x3, blocking collectives, local(): liabilities = lax.psum(liab_part, ('pol', 'fund'))  85 us
    while x32, local copies, waits for them, and re-layouts  72 us
    dot_general x12, matrix products, move_block(): lax.dot_general(credited, onehot, contract_rows, precision=highest, prefe...  36.4 us
    psum x1, waiting for transfers between devices, local(): lax.psum(jnp.stack([asset_part(month_num) for month_num in range(months)]...  24.1 us
    dot_general x8, matrix products, move_block(): lax.dot_general(onehot, force_new * account_new, contract_cols, precision...  16.2 us
  transfers between devices with their start and end apart: 1, of which 1 were waited for; matrix products, arithmetic and copies ran while one was open for 1% of the time, Pallas kernels for 0%

commit v1 on v0

v1 whole, which is shorter than its diff:
```python
import functools

import jax
import jax.numpy as jnp
from jax import lax
from jax.experimental import pallas as pl
from jax.experimental.pallas import tpu as pltpu
from jax.sharding import PartitionSpec as P

surrender_end = 84
lanes = 128
f32, bf16 = jnp.float32, jnp.bfloat16
contract_cols = (((1,), (1,)), ((), ()))


def round_up(value, unit):
    return -(-value // unit) * unit


def split(value):
    high = value.astype(bf16)
    return high, (value - high.astype(f32)).astype(bf16)


def dot(left, right):
    return jnp.dot(left, right, preferred_element_type=f32)


def dot_cols(left, right):
    return lax.dot_general(left, right, contract_cols, preferred_element_type=f32)


def onehot(ids_row, row_count):
    rows = lax.broadcasted_iota(jnp.int32, (row_count, ids_row.shape[1]), 0)
    return rows == ids_row


def gather_kernel(
    group,
    months,
    kinds,
    funds,
    count_ref,
    value_ref,
    dur_ref,
    prod_ref,
    pfund_ref,
    flows_ref,
    bfund_ref,
    hold_ref,
    out_ref,
    part_buf,
    recv_buf,
    sum_buf,
    send_a,
    recv_a,
    send_b,
    recv_b,
):
    pol_devs, fund_devs = group
    n = pol_devs * fund_devs
    me = lax.axis_index("pol") * fund_devs + lax.axis_index("fund")

    def peer_of(step):
        peer = lax.rem(me + step, n)
        return peer, {"pol": peer // fund_devs, "fund": lax.rem(peer, fund_devs)}

    barrier = pltpu.get_barrier_semaphore()
    for step in range(1, n):
        pl.semaphore_signal(
            barrier, inc=1, device_id=peer_of(step)[1], device_id_type=pl.DeviceIdType.MESH
        )

    wide = part_buf.shape[2]
    chunk = part_buf.shape[1]
    part_buf[...] = jnp.zeros_like(part_buf)

    held = jnp.where(onehot(bfund_ref[...], funds), hold_ref[...], 0.0)
    held_h, held_l = split(held)
    flow_h, flow_l = split(flows_ref[...])
    weights = dot_cols(held_h, flow_h) + (
        dot_cols(held_h, flow_l) + dot_cols(held_l, flow_h)
    )

    worth = count_ref[...] * value_ref[...]
    late = jnp.clip(dur_ref[...] - (surrender_end - (months - 1)), 0, months - 1)
    kind = late * kinds + prod_ref[...]
    classed = jnp.where(onehot(kind, months * kinds), worth, 0.0)
    pol_hot = onehot(pfund_ref[...], wide).astype(f32).astype(bf16)
    worth_h, worth_l = split(classed)
    classes = dot_cols(worth_h, pol_hot) + dot_cols(worth_l, pol_hot)

    def put(values, first):
        row = first
        while row < first + values.shape[0]:
            slot, inner = row // chunk, row % chunk
            size = min(chunk - inner, first + values.shape[0] - row)
            part_buf[slot, inner : inner + size, : values.shape[1]] = values[
                row - first : row - first + size
            ]
            row += size

    put(weights, 0)
    put(classes, funds)

    pl.semaphore_wait(barrier, n - 1)

    def scatter(step):
        peer, where = peer_of(step)
        return pltpu.make_async_remote_copy(
            src_ref=part_buf.at[peer],
            dst_ref=recv_buf.at[me],
            send_sem=send_a.at[peer],
            recv_sem=recv_a.at[me],
            device_id=where,
            device_id_type=pl.DeviceIdType.MESH,
        )

    def spread(step):
        peer, where = peer_of(step)
        return pltpu.make_async_remote_copy(
            src_ref=sum_buf.at[me],
            dst_ref=sum_buf.at[me],
            send_sem=send_b.at[peer],
            recv_sem=recv_b.at[me],
            device_id=where,
            device_id_type=pl.DeviceIdType.MESH,
        )

    def arrival(buf, sems, step):
        peer, where = peer_of(step)
        return pltpu.make_async_remote_copy(
            src_ref=buf.at[peer],
            dst_ref=buf.at[peer],
            send_sem=send_a.at[peer],
            recv_sem=sems.at[peer],
            device_id=where,
            device_id_type=pl.DeviceIdType.MESH,
        )

    for step in range(1, n):
        scatter(step).start()
    total = part_buf[me]
    for step in range(1, n):
        arrival(recv_buf, recv_a, step).wait_recv()
        total = total + recv_buf[peer_of(step)[0]]
    sum_buf[me] = total
    for step in range(1, n):
        spread(step).start()
    for step in range(1, n):
        arrival(sum_buf, recv_b, step).wait_recv()
    for slot in range(n):
        out_ref[slot * chunk : (slot + 1) * chunk, :] = sum_buf[slot]
    for step in range(1, n):
        scatter(step).wait_send()
        spread(step).wait_send()


def project_kernel(
    months,
    kinds,
    funds,
    block,
    base_ref,
    sens_ref,
    fee_ref,
    share_ref,
    sums_ref,
    rates_ref,
    count_ref,
    value_ref,
    dur_ref,
    prod_ref,
    pfund_ref,
    cred_ref,
    out_ref,
    table,
    gathered,
    rows,
    market_sum,
    staged,
    out_sems,
):
    tenors = rates_ref.shape[1]
    scen = rates_ref.shape[2]
    wide = sums_ref.shape[1]
    policies = count_ref.shape[1]

    products = prod_ref[...]
    base = jnp.zeros(products.shape, f32)
    sens = base
    fee = base
    for k in range(kinds):
        match = products == k
        base = jnp.where(match, base_ref[k], base)
        sens = jnp.where(match, sens_ref[k], sens)
        fee = jnp.where(match, fee_ref[k], fee)
    rows[0:1, :] = count_ref[...] * value_ref[...]
    rows[1:2, :] = sens
    rows[2:3, :] = -float(months) * fee
    for t in range(months):
        rows[3 + t : 4 + t, :] = -jnp.where(dur_ref[...] + t >= surrender_end, 2.0, 1.0) * base

    tenor_years = (
        lax.broadcasted_iota(jnp.int32, (1, tenors), 1).astype(f32) + 1.0
    ) / 12.0
    weights = sums_ref[0:funds, 0:tenors]
    weight_h, weight_l = split(weights)
    start = [
        [sums_ref[funds + u * kinds + k : funds + u * kinds + k + 1, :] for k in range(kinds)]
        for u in range(months)
    ]
    exp_fee = [jnp.exp(jnp.full((1, wide), -fee_ref[k], f32)) for k in range(kinds)]
    lane = lax.broadcasted_iota(jnp.int32, (scen, wide), 1)
    share = share_ref[...]
    if wide > funds:
        share = jnp.concatenate([share, jnp.zeros((1, wide - funds), f32)], axis=1)
    factors = None
    growth = None
    for t in range(months):
        rates = rates_ref[t].T
        disc_h, disc_l = split(jnp.exp(-rates * tenor_years))
        assets = dot_cols(disc_h, weight_h) + (
            dot_cols(disc_h, weight_l) + dot_cols(disc_l, weight_h)
        )
        if wide > funds:
            assets = jnp.concatenate([assets, jnp.ones((scen, wide - funds), f32)], axis=1)
        if factors is None:
            liab = functools.reduce(jnp.add, [w for line in start for w in line])
        else:
            parts = [
                start[u][k] * factors[u][k] for u in range(months) for k in range(kinds)
            ]
            liab = functools.reduce(jnp.add, parts) * jnp.exp(growth)
        credited = jnp.where(lane < funds, share * jnp.log(assets / liab), 0.0)
        cred_ref[t] = credited.T[:funds]
        market = rates[:, tenors - 1 : tenors]
        spread = market - credited
        table[t * scen : (t + 1) * scen, 0:wide] = spread.astype(bf16)
        table[t * scen : (t + 1) * scen, wide : 2 * wide] = split(spread)[1]
        market_all = market if t == 0 else market_all + market
        growth = credited / 12.0 if t == 0 else growth + credited / 12.0
        if t < months - 1:
            stay = [jnp.exp(-base_ref[k] * jnp.exp(sens_ref[k] * spread)) for k in range(kinds)]
            new = []
            for u in range(months):
                line = []
                for k in range(kinds):
                    step = stay[k] * stay[k] if u >= months - 1 - t else stay[k]
                    line.append(step if factors is None else factors[u][k] * step)
                new.append(line)
            factors = new
            start = [[start[u][k] * exp_fee[k] for k in range(kinds)] for u in range(months)]
    market_sum[...] = jnp.broadcast_to(market_all / 12.0, (scen, lanes))

    tile = min(scen, 32)

    def out_copy(idx):
        cols = pl.ds(pl.multiple_of(idx * block, block), block)
        return pltpu.make_async_copy(staged.at[idx], out_ref.at[:, cols], out_sems.at[idx])

    @pl.loop(0, policies // block)
    def _(idx):
        cols = pl.ds(pl.multiple_of(idx * block, block), block)
        hot = jnp.where(onehot(pfund_ref[:, cols], wide), 1.0, 0.0).astype(bf16)
        gathered[...] = dot(table[...], jnp.concatenate([hot, hot], axis=0))
        worth = rows[0:1, cols]
        sens_row = rows[1:2, cols]
        fee_row = rows[2:3, cols]
        for first in range(0, scen, tile):
            acc = fee_row + jnp.tile(market_sum[first : first + tile, :], (1, block // lanes))
            spread_sum = None
            for t in range(months):
                spread = gathered[t * scen + first : t * scen + first + tile, :]
                acc = acc + rows[3 + t : 4 + t, cols] * jnp.exp(sens_row * spread)
                spread_sum = spread if t == 0 else spread_sum + spread
            staged[idx, first : first + tile, :] = worth * jnp.exp(
                acc - spread_sum * (1.0 / 12.0)
            )
        out_copy(idx).start()

    @pl.loop(0, policies // block)
    def _(idx):
        out_copy(idx).wait()


def local(
    group,
    count_init,
    value_init,
    durations,
    products,
    policy_fund,
    lapse_base,
    lapse_sens,
    fee_rate,
    fund_share,
    bond_flows,
    bond_fund,
    holdings,
    scen_rates,
):
    funds = fund_share.shape[0]
    months, tenors, scen = scen_rates.shape
    kinds = lapse_base.shape[0]
    policies = count_init.shape[0]
    n = group[0] * group[1]
    wide = round_up(max(funds, tenors), lanes)
    chunk = -(-(funds + months * kinds) // n)
    vmem = pl.BlockSpec(memory_space=pltpu.VMEM)
    smem = pl.BlockSpec(memory_space=pltpu.SMEM)
    count_row, value_row, dur_row, prod_row, pfund_row, bfund_row, hold_row = (
        x[None, :]
        for x in (
            count_init,
            value_init,
            durations,
            products,
            policy_fund,
            bond_fund,
            holdings,
        )
    )
    sums = pl.pallas_call(
        functools.partial(gather_kernel, group, months, kinds, funds),
        out_shape=jax.ShapeDtypeStruct((n * chunk, wide), f32),
        in_specs=[vmem] * 8,
        out_specs=vmem,
        scratch_shapes=[
            pltpu.VMEM((n, chunk, wide), f32),
            pltpu.VMEM((n, chunk, wide), f32),
            pltpu.VMEM((n, chunk, wide), f32),
            pltpu.SemaphoreType.DMA((n,)),
            pltpu.SemaphoreType.DMA((n,)),
            pltpu.SemaphoreType.DMA((n,)),
            pltpu.SemaphoreType.DMA((n,)),
        ],
        compiler_params=pltpu.CompilerParams(collective_id=0, has_side_effects=True),
        name="fund_sums",
    )(
        count_row,
        value_row,
        dur_row,
        prod_row,
        pfund_row,
        bond_flows.T,
        bfund_row,
        hold_row,
    )
    block = 256 if policies % 256 == 0 else policies
    return pl.pallas_call(
        functools.partial(project_kernel, months, kinds, funds, block),
        out_shape=(
            jax.ShapeDtypeStruct((months, funds, scen), f32),
            jax.ShapeDtypeStruct((scen, policies), f32),
        ),
        in_specs=[smem] * 3 + [vmem] * 8,
        out_specs=(vmem, pl.BlockSpec(memory_space=pl.ANY)),
        scratch_shapes=[
            pltpu.VMEM((months * scen, 2 * wide), bf16),
            pltpu.VMEM((months * scen, block), f32),
            pltpu.VMEM((round_up(3 + months, 8), policies), f32),
            pltpu.VMEM((scen, lanes), f32),
            pltpu.VMEM((policies // block, scen, block), f32),
            pltpu.SemaphoreType.DMA((policies // block,)),
        ],
        name="project",
    )(
        lapse_base,
        lapse_sens,
        fee_rate,
        fund_share[None, :],
        sums,
        scen_rates,
        count_row,
        value_row,
        dur_row,
        prod_row,
        pfund_row,
    )


def solution(mesh):
    in_specs = (
        P(("pol", "fund")),
        P(("pol", "fund")),
        P(("pol", "fund")),
        P(("pol", "fund")),
        P(("pol", "fund")),
        P(),
        P(),
        P(),
        P(),
        P(("pol", "fund"), None),
        P(("pol", "fund")),
        P(("pol", "fund")),
        P(None, None, ("parts", "scen")),
    )
    out_specs = (P(None, None, ("parts", "scen")), P(("parts", "scen"), ("pol", "fund")))
    group = (mesh.shape["pol"], mesh.shape["fund"])
    return jax.shard_map(
        functools.partial(local, group),
        mesh=mesh,
        in_specs=in_specs,
        out_specs=out_specs,
        check_vma=False,
    )
```

time: 274 us -> 23.6 us (0.09)
  blocking collectives: 85 us -> 0 us
  local copies, waits for them, and re-layouts: 81 us -> 0 us
  matrix products: 60 us -> 0 us
  waiting for transfers between devices: 24.1 us -> 0 us
  Pallas kernels: 0 us -> 22.8 us
  between operations: 14.4 us -> 0.64 us
  other arithmetic: 7.53 us -> 0 us
    psum x3 -> x0, blocking collectives: 85 us -> none  [local(): liabilities = lax.psum(liab_part, ('pol', 'fund'))]
    while x34 -> x0, local copies, waits for them, and re-layouts: 76.9 us -> none
    dot_general x30 -> x0, matrix products: 60 us -> none  [the longest x12 36.4 us: move_block(): lax.dot_general(credited, onehot, contract_rows, precision=highest, prefe...]
    psum x1 -> x0, waiting for transfers between devices: 24.1 us -> none  [local(): lax.psum(jnp.stack([asset_part(month_num) for month_num in range(months)]...]
    pallas_call x0 -> x2, Pallas kernels: none -> 22.8 us  [the longest x1 14.8 us: local(): pl.pallas_call(functools.partial(gather_kernel, group, months, kinds, fun...]
    mul x17 -> x0, other arithmetic: 5.96 us -> none  [the longest x1 3.13 us: local(): return (jnp.stack(credited_list), in_force * account)]
  transfers between devices with their start and end apart: 1 -> 0, of which waited for: 1 -> 0; matrix products, arithmetic and copies ran while one was open for 1% -> 0% of each run, Pallas kernels for 0% -> 0%
where the time goes in v1:
time: 23.6 us; the launch traced here: 23.4 us
  Pallas kernels  22.8 us (97%)
  between operations  0.64 us (3%)
    pallas_call x1, Pallas kernels, local(): pl.pallas_call(functools.partial(gather_kernel, group, months, kinds, fun...  14.8 us
    pallas_call x1, Pallas kernels, local(): pl.pallas_call(functools.partial(project_kernel, months, kinds, funds, bl...  7.96 us

profile of v1, /device:TPU:0, one launch (start us, length us, event | category | flops | bytes accessed | tf_op | source)
XLA Modules:
  0.0 23.4 jit_solution(1681862442216916640)
XLA Ops:
  0.6 14.8 %fund_sums.1.sums_ref = f32[144,128]{1,0:T(8,128)} custom-call(f32[1,4096]{1,0:T(1,128)} %bitcast.10, f32[1,4096]{1,0:T(1,128)} %bitcast.12, s32[1,4096]{1,0:T(1,128)} %bitcast.14, s32[1,4096]{1,0:T(1,128)} %bitcast.16, s32[1,4096]{1,0:T(1,128)} %bitcast.18, f32[120,2048]{1,0:T(8,128)} %bitcast.9, s32[1,2048]{1,0:T(1,128)} %bitcast.20, f32[1,2048]{1,0:T(1,128)} %bitcast.21), custom_call_target="tpu_custom_call" | custom-call | tf_op jit(solution)/shard_map/fund_sums/pallas_call | solution.py:324
  15.5 8.0 %project.1 = (f32[3,120,128]{2,1,0:T(8,128)}, f32[128,4096]{1,0:T(8,128)}) custom-call(f32[8]{0:T(128)} %base_ref.1, f32[8]{0:T(128)} %sens_ref.1, f32[8]{0:T(128)} %fee_ref.1, f32[1,120]{1,0:T(1,128)} %bitcast.22, f32[144,128]{1,0:T(8,128)} %fund_sums.1.sums_ref, f32[3,120,128]{2,1,0:T(8,128)} %rates_ref.1, f32[1,4096]{1,0:T(1,128)} %bitcast.11, ...), custom_call_target="tpu_custom_call" | custom-call | tf_op jit(solution)/shard_map/project/pallas_call | solution.py:351

commit v2 on v1

v2 whole, which is shorter than its diff:
```python
import functools

import jax
import jax.numpy as jnp
from jax import lax
from jax.experimental import pallas as pl
from jax.experimental.pallas import tpu as pltpu
from jax.sharding import PartitionSpec as P

surrender_end = 84
lanes = 128
log2_e = 1.4426950408889634
f32, bf16 = jnp.float32, jnp.bfloat16
contract_cols = (((1,), (1,)), ((), ()))


def round_up(value, unit):
    return -(-value // unit) * unit


def split(value):
    high = value.astype(bf16)
    return high, (value - high.astype(f32)).astype(bf16)


def dot(left, right):
    return jnp.dot(left, right, preferred_element_type=f32)


def dot_cols(left, right):
    return lax.dot_general(left, right, contract_cols, preferred_element_type=f32)


def onehot(ids_row, values, row_count):
    shape = (16, ids_row.shape[1])
    kind = bf16 if row_count <= 256 else f32
    ids = jnp.broadcast_to(ids_row.astype(f32), shape).astype(kind)
    rows = lax.broadcasted_iota(jnp.int32, shape, 0).astype(f32)
    values = [jnp.broadcast_to(v, shape).astype(bf16) for v in values]
    masks = [ids == (rows + float(g)).astype(kind) for g in range(0, row_count, 16)]
    zero = jnp.zeros(shape, bf16)
    return [jnp.concatenate([jnp.where(m, v, zero) for m in masks], axis=0) for v in values]


def split_row(row):
    high = row.astype(bf16).astype(f32)
    return high, row - high


def gather_kernel(
    group,
    kinds,
    funds,
    bfund_hbm,
    hold_hbm,
    flows_hbm,
    pfund_hbm,
    count_hbm,
    value_hbm,
    dur_hbm,
    prod_hbm,
    base_hbm,
    sens_hbm,
    fee_hbm,
    share_hbm,
    rates_hbm,
    out_ref,
    hot_ref,
    rows_ref,
    disc_ref,
    market_ref,
    kind_ref,
    share_ref,
    bfund_ref,
    hold_ref,
    flows_ref,
    pfund_ref,
    count_ref,
    value_ref,
    dur_ref,
    prod_ref,
    base_ref,
    sens_ref,
    fee_ref,
    rates_ref,
    in_sems,
    part_buf,
    recv_buf,
    sum_buf,
    send_a,
    recv_a,
    send_b,
    recv_b,
):
    pol_devs, fund_devs = group
    n = pol_devs * fund_devs
    pairs = (
        (bfund_hbm, bfund_ref),
        (hold_hbm, hold_ref),
        (flows_hbm, flows_ref),
        (pfund_hbm, pfund_ref),
        (count_hbm, count_ref),
        (value_hbm, value_ref),
        (dur_hbm, dur_ref),
        (prod_hbm, prod_ref),
        (base_hbm, base_ref),
        (sens_hbm, sens_ref),
        (fee_hbm, fee_ref),
        (share_hbm, share_ref),
        (rates_hbm, rates_ref),
    )
    loads = [
        pltpu.make_async_copy(src, dst, in_sems.at[i]) for i, (src, dst) in enumerate(pairs)
    ]
    for load in loads:
        load.start()
    me = lax.axis_index("pol") * fund_devs + lax.axis_index("fund")

    def peer_of(step):
        peer = lax.rem(me + step, n)
        return peer, {"pol": peer // fund_devs, "fund": lax.rem(peer, fund_devs)}

    barrier = pltpu.get_barrier_semaphore()
    for step in range(1, n):
        pl.semaphore_signal(
            barrier, inc=1, device_id=peer_of(step)[1], device_id_type=pl.DeviceIdType.MESH
        )

    months, tenors, scen = rates_ref.shape
    wide = part_buf.shape[2]
    chunk = part_buf.shape[1]
    part_buf[...] = jnp.zeros_like(part_buf)

    for load in loads[:3]:
        load.wait()
    flows = flows_ref[...]
    if wide > tenors:
        flows = jnp.concatenate(
            [flows, jnp.zeros((wide - tenors, flows.shape[1]), f32)], axis=0
        )
    held = jnp.concatenate(onehot(bfund_ref[...], split_row(hold_ref[...]), wide), axis=0)
    quads = dot_cols(held, jnp.concatenate(split(flows), axis=0))
    weights = (quads[:funds, :wide] + quads[wide : wide + funds, wide:]) + (
        quads[:funds, wide:] + quads[wide : wide + funds, :wide]
    )

    for load in loads[3:8]:
        load.wait()
    worth = count_ref[...] * value_ref[...]
    late = jnp.clip(dur_ref[...] - (surrender_end - (months - 1)), 0, months - 1)
    kind = late * kinds + prod_ref[...]
    classed = onehot(kind, split_row(worth), round_up(months * kinds, 16))
    (pol_hot,) = onehot(pfund_ref[...], [jnp.ones(worth.shape, f32)], wide)
    hot_ref[...] = pol_hot
    sides = dot_cols(jnp.concatenate(classed, axis=0), pol_hot)
    half = sides.shape[0] // 2
    classes = (sides[:half] + sides[half:])[: months * kinds]

    def put(values, first):
        row = first
        while row < first + values.shape[0]:
            slot, inner = row // chunk, row % chunk
            size = min(chunk - inner, first + values.shape[0] - row)
            part_buf[slot, inner : inner + size, : values.shape[1]] = values[
                row - first : row - first + size
            ]
            row += size

    put(weights, 0)
    put(classes, funds)

    pl.semaphore_wait(barrier, n - 1)

    def scatter(step):
        peer, where = peer_of(step)
        return pltpu.make_async_remote_copy(
            src_ref=part_buf.at[peer],
            dst_ref=recv_buf.at[me],
            send_sem=send_a.at[peer],
            recv_sem=recv_a.at[me],
            device_id=where,
            device_id_type=pl.DeviceIdType.MESH,
        )

    def spread(step):
        peer, where = peer_of(step)
        return pltpu.make_async_remote_copy(
            src_ref=sum_buf.at[me],
            dst_ref=sum_buf.at[me],
            send_sem=send_b.at[peer],
            recv_sem=recv_b.at[me],
            device_id=where,
            device_id_type=pl.DeviceIdType.MESH,
        )

    def arrival(buf, sems, step):
        peer, where = peer_of(step)
        return pltpu.make_async_remote_copy(
            src_ref=buf.at[peer],
            dst_ref=buf.at[peer],
            send_sem=send_a.at[peer],
            recv_sem=sems.at[peer],
            device_id=where,
            device_id_type=pl.DeviceIdType.MESH,
        )

    for step in range(1, n):
        scatter(step).start()

    for load in loads[8:]:
        load.wait()
    for k in range(kinds):
        kind_ref[k : k + 1, :] = jnp.full((1, wide), -log2_e * base_ref[k], f32)
        kind_ref[kinds + k : kinds + k + 1, :] = jnp.full((1, wide), 12.0 * sens_ref[k], f32)
        kind_ref[2 * kinds + k : 2 * kinds + k + 1, :] = jnp.exp(
            jnp.full((1, wide), -fee_ref[k], f32)
        )
    products = prod_ref[...]
    base = jnp.zeros(products.shape, f32)
    sens = base
    fee = base
    for k in range(kinds):
        match = products == k
        base = jnp.where(match, base_ref[k], base)
        sens = jnp.where(match, sens_ref[k], sens)
        fee = jnp.where(match, fee_ref[k], fee)
    rows_ref[0:1, :] = jnp.log2(worth) - (months * log2_e) * fee
    rows_ref[1:2, :] = 12.0 * sens
    for t in range(months):
        rows_ref[2 + t : 3 + t, :] = base * jnp.where(
            dur_ref[...] + t >= surrender_end, -2.0 * log2_e, -log2_e
        )

    total = part_buf[me]
    for step in range(1, n):
        arrival(recv_buf, recv_a, step).wait_recv()
        total = total + recv_buf[peer_of(step)[0]]
    sum_buf[me] = total
    for step in range(1, n):
        spread(step).start()

    tenor_years = (
        lax.broadcasted_iota(jnp.int32, (1, tenors), 1).astype(f32) + 1.0
    ) / 12.0
    disc_ref[...] = jnp.zeros_like(disc_ref)
    for t in range(months):
        rates = rates_ref[t].T
        disc_h, disc_l = split(jnp.exp(-rates * tenor_years))
        span = slice(t * scen, (t + 1) * scen)
        disc_ref[span, 0:tenors] = disc_h
        disc_ref[span, wide : wide + tenors] = disc_l
        market_ref[span, :] = jnp.broadcast_to(rates[:, tenors - 1 : tenors], (scen, wide))

    for step in range(1, n):
        arrival(sum_buf, recv_b, step).wait_recv()
    for slot in range(n):
        out_ref[slot * chunk : (slot + 1) * chunk, :] = sum_buf[slot]
    for step in range(1, n):
        scatter(step).wait_send()
        spread(step).wait_send()


def project_kernel(
    kinds,
    funds,
    block,
    sums_ref,
    hot_ref,
    rows,
    disc_ref,
    market_ref,
    kind_ref,
    share_ref,
    cred_ref,
    out_ref,
    table,
    assets_buf,
    gathered,
    market_sum,
    staged,
    out_sems,
):
    months = cred_ref.shape[0]
    scen = cred_ref.shape[2]
    wide = sums_ref.shape[1]
    policies = hot_ref.shape[1]

    weights = sums_ref[0:funds, :]
    if wide > funds:
        weights = jnp.concatenate([weights, jnp.zeros((wide - funds, wide), f32)], axis=0)
    weight_h, weight_l = split(weights)
    both = jnp.concatenate(
        [
            jnp.concatenate([weight_h, weight_h], axis=1),
            jnp.concatenate([weight_l, weight_l], axis=1),
        ],
        axis=0,
    )
    halves = dot_cols(disc_ref[...], both)
    assets_buf[...] = halves[:, :wide] + halves[:, wide:]

    base_rows, sens_rows, exp_fee = (
        [kind_ref[i * kinds + k : i * kinds + k + 1, :] for k in range(kinds)] for i in range(3)
    )
    start = [
        [[sums_ref[funds + u * kinds + k : funds + u * kinds + k + 1, :] for k in range(kinds)]
         for u in range(months)]
    ]
    for t in range(1, months):
        start.append([[w * e for w, e in zip(line, exp_fee)] for line in start[-1]])
    share = share_ref[...]
    if wide > funds:
        share = jnp.concatenate([share, jnp.zeros((1, wide - funds), f32)], axis=1)

    tile = min(scen, 32)
    lane = lax.broadcasted_iota(jnp.int32, (tile, wide), 1)
    for first in range(0, scen, tile):
        stays = []
        growth = None
        market_all = None
        for t in range(months):
            span = slice(t * scen + first, t * scen + first + tile)
            liab = None
            for k in range(kinds):
                acc = start[t][months - 1][k]
                for u in range(months - 1, 0, -1):
                    early = months - 1 - u
                    if early < t:
                        acc = acc * stays[early][k]
                    acc = acc + start[t][u - 1][k]
                for early in range(t):
                    acc = acc * stays[early][k]
                liab = acc if liab is None else liab + acc
            if growth is not None:
                liab = liab * jnp.exp2(growth)
            ratio = jnp.where(lane < funds, assets_buf[span, :] / liab, 1.0)
            credited = share * jnp.log(ratio)
            cred_ref[t, :, first : first + tile] = credited.T[:funds]
            market = market_ref[span, :]
            scaled = (market - credited) * (log2_e / 12.0)
            high, low = split(scaled)
            table[span, 0:wide] = high
            table[span, wide : 2 * wide] = low
            moved = credited * (log2_e / 12.0)
            growth = moved if growth is None else growth + moved
            market_all = market if market_all is None else market_all + market
            if t < months - 1:
                stays.append(
                    [
                        jnp.exp2(base_rows[k] * jnp.exp2(sens_rows[k] * scaled))
                        for k in range(kinds)
                    ]
                )
        market_sum[first : first + tile, :] = market_all[:, :lanes] * (log2_e / 12.0)

    def out_copy(idx):
        cols = pl.ds(pl.multiple_of(idx * block, block), block)
        return pltpu.make_async_copy(staged.at[idx], out_ref.at[:, cols], out_sems.at[idx])

    def fetch(idx, slot):
        cols = pl.ds(pl.multiple_of(idx * block, block), block)
        hot = hot_ref[:, cols]
        gathered[slot] = dot(table[...], jnp.concatenate([hot, hot], axis=0))

    def settle(idx, slot):
        cols = pl.ds(pl.multiple_of(idx * block, block), block)
        first_row = rows[0:1, cols]
        sens_row = rows[1:2, cols]
        for first in range(0, scen, tile):
            acc = first_row + jnp.tile(market_sum[first : first + tile, :], (1, block // lanes))
            for t in range(months):
                spread = gathered[slot, t * scen + first : t * scen + first + tile, :]
                acc = acc + (rows[2 + t : 3 + t, cols] * jnp.exp2(sens_row * spread) - spread)
            staged[idx, first : first + tile, :] = jnp.exp2(acc)
        out_copy(idx).start()

    blocks = policies // block
    fetch(0, 0)

    @pl.loop(0, blocks, step=2)
    def _(idx):
        fetch(idx + 1, 1)
        settle(idx, 0)
        fetch(jnp.minimum(idx + 2, blocks - 1), 0)
        settle(idx + 1, 1)

    @pl.loop(0, blocks)
    def _(idx):
        out_copy(idx).wait()


def local(
    group,
    count_init,
    value_init,
    durations,
    products,
    policy_fund,
    lapse_base,
    lapse_sens,
    fee_rate,
    fund_share,
    bond_flows,
    bond_fund,
    holdings,
    scen_rates,
):
    funds = fund_share.shape[0]
    months, tenors, scen = scen_rates.shape
    kinds = lapse_base.shape[0]
    policies = count_init.shape[0]
    n = group[0] * group[1]
    wide = round_up(max(funds, tenors), lanes)
    chunk = -(-(funds + months * kinds) // n)
    vmem = pl.BlockSpec(memory_space=pltpu.VMEM)
    count_row, value_row, dur_row, prod_row, pfund_row, bfund_row, hold_row = (
        x[None, :]
        for x in (
            count_init,
            value_init,
            durations,
            products,
            policy_fund,
            bond_fund,
            holdings,
        )
    )
    few = 24 << 20
    hbm = pl.BlockSpec(memory_space=pltpu.HBM)
    sources = (
        bfund_row,
        hold_row,
        bond_flows.T,
        pfund_row,
        count_row,
        value_row,
        dur_row,
        prod_row,
        lapse_base,
        lapse_sens,
        fee_rate,
        fund_share[None, :],
        scen_rates,
    )
    carried = pl.pallas_call(
        functools.partial(gather_kernel, group, kinds, funds),
        out_shape=(
            jax.ShapeDtypeStruct((n * chunk, wide), f32),
            jax.ShapeDtypeStruct((wide, policies), bf16),
            jax.ShapeDtypeStruct((round_up(2 + months, 8), policies), f32),
            jax.ShapeDtypeStruct((months * scen, 2 * wide), bf16),
            jax.ShapeDtypeStruct((months * scen, wide), f32),
            jax.ShapeDtypeStruct((3 * kinds, wide), f32),
            jax.ShapeDtypeStruct((1, funds), f32),
        ),
        in_specs=[hbm] * len(sources),
        out_specs=(vmem,) * 7,
        scratch_shapes=[
            *(pltpu.VMEM(x.shape, x.dtype) for x in sources[:8]),
            *(pltpu.SMEM(x.shape, x.dtype) for x in sources[8:11]),
            pltpu.VMEM(scen_rates.shape, f32),
            pltpu.SemaphoreType.DMA((len(sources),)),
            pltpu.VMEM((n, chunk, wide), f32),
            pltpu.VMEM((n, chunk, wide), f32),
            pltpu.VMEM((n, chunk, wide), f32),
            pltpu.SemaphoreType.DMA((n,)),
            pltpu.SemaphoreType.DMA((n,)),
            pltpu.SemaphoreType.DMA((n,)),
            pltpu.SemaphoreType.DMA((n,)),
        ],
        compiler_params=pltpu.CompilerParams(
            collective_id=0, has_side_effects=True, vmem_limit_bytes=few
        ),
        name="fund_sums",
    )(*(pltpu.with_memory_space_constraint(x, pltpu.HBM) for x in sources))
    block = policies // (2 * max(1, policies // 512))
    return pl.pallas_call(
        functools.partial(project_kernel, kinds, funds, block),
        out_shape=(
            jax.ShapeDtypeStruct((months, funds, scen), f32),
            jax.ShapeDtypeStruct((scen, policies), f32),
        ),
        in_specs=[vmem] * 7,
        out_specs=(vmem, pl.BlockSpec(memory_space=pl.ANY)),
        scratch_shapes=[
            pltpu.VMEM((months * scen, 2 * wide), bf16),
            pltpu.VMEM((months * scen, wide), f32),
            pltpu.VMEM((2, months * scen, block), f32),
            pltpu.VMEM((scen, lanes), f32),
            pltpu.VMEM((policies // block, scen, block), f32),
            pltpu.SemaphoreType.DMA((policies // block,)),
        ],
        compiler_params=pltpu.CompilerParams(vmem_limit_bytes=few),
        name="project",
    )(*carried)


def solution(mesh):
    in_specs = (
        P(("pol", "fund")),
        P(("pol", "fund")),
        P(("pol", "fund")),
        P(("pol", "fund")),
        P(("pol", "fund")),
        P(),
        P(),
        P(),
        P(),
        P(("pol", "fund"), None),
        P(("pol", "fund")),
        P(("pol", "fund")),
        P(None, None, ("parts", "scen")),
    )
    out_specs = (P(None, None, ("parts", "scen")), P(("parts", "scen"), ("pol", "fund")))
    group = (mesh.shape["pol"], mesh.shape["fund"])
    return jax.shard_map(
        functools.partial(local, group),
        mesh=mesh,
        in_specs=in_specs,
        out_specs=out_specs,
        check_vma=False,
    )
```

time: 23.6 us -> 19 us (0.81)
  Pallas kernels: 22.8 us -> 18.2 us
    pallas_call x2, Pallas kernels: 22.8 us -> 18.2 us  [the longest x1 13.2 us: local(): pl.pallas_call(functools.partial(gather_kernel, group, kinds, funds), out...]
where the time goes in v2:
time: 19 us; the launch traced here: 18.8 us
  Pallas kernels  18.2 us (96%)
  between operations  0.64 us (3%)
    pallas_call x1, Pallas kernels, local(): pl.pallas_call(functools.partial(gather_kernel, group, kinds, funds), out...  13.2 us
    pallas_call x1, Pallas kernels, local(): pl.pallas_call(functools.partial(project_kernel, kinds, funds, block), ou...  5.04 us

profile of v2, /device:TPU:0, one launch (start us, length us, event | category | flops | bytes accessed | tf_op | source)
XLA Modules:
  0.0 18.8 jit_solution(1953633208389287591)
XLA Ops:
  0.6 13.2 %fund_sums.1 = (f32[144,128]{1,0:T(8,128)S(1)}, bf16[128,4096]{1,0:T(8,128)(2,1)S(1)}, f32[8,4096]{1,0:T(8,128)S(1)}, bf16[384,256]{1,0:T(8,128)(2,1)S(1)}, f32[...) custom-call(s32[1,2048]{1,0:T(1,128)} %bitcast.15, f32[1,2048]{1,0:T(1,128)} %bitcast.16, ...), custom_call_target="tpu_custom_call" | custom-call | tf_op jit(solution)/shard_map/fund_sums/pallas_call | solution.py:445
  13.8 5.0 %project.1 = (f32[3,120,128]{2,1,0:T(8,128)}, f32[128,4096]{1,0:T(8,128)}) custom-call(f32[144,128]{1,0:T(8,128)S(1)} %get-tuple-element.9.sums_ref, bf16[128,4096]{1,0:T(8,128)(2,1)S(1)} %get-tuple-element.10.hot_ref, f32[8,4096]{1,0:T(8,128)S(1)} %get-tuple-element.11.rows, bf16[384,256]{1,0:T(8,128)(2,1)S(1)} %get-tuple-element.12.disc_ref, ...), custom_call_target="tpu_custom_call" | custom-call | tf_op jit(solution)/shard_map/project/pallas_call | solution.py:477

commit v3 on v2

--- a/solution.py
+++ b/solution.py
@@ -131,19 +131,6 @@
     chunk = part_buf.shape[1]
     part_buf[...] = jnp.zeros_like(part_buf)
 
-    for load in loads[:3]:
-        load.wait()
-    flows = flows_ref[...]
-    if wide > tenors:
-        flows = jnp.concatenate(
-            [flows, jnp.zeros((wide - tenors, flows.shape[1]), f32)], axis=0
-        )
-    held = jnp.concatenate(onehot(bfund_ref[...], split_row(hold_ref[...]), wide), axis=0)
-    quads = dot_cols(held, jnp.concatenate(split(flows), axis=0))
-    weights = (quads[:funds, :wide] + quads[wide : wide + funds, wide:]) + (
-        quads[:funds, wide:] + quads[wide : wide + funds, :wide]
-    )
-
     for load in loads[3:8]:
         load.wait()
     worth = count_ref[...] * value_ref[...]
@@ -155,6 +142,19 @@
     sides = dot_cols(jnp.concatenate(classed, axis=0), pol_hot)
     half = sides.shape[0] // 2
     classes = (sides[:half] + sides[half:])[: months * kinds]
+
+    for load in loads[:3]:
+        load.wait()
+    flows = flows_ref[...]
+    if wide > tenors:
+        flows = jnp.concatenate(
+            [flows, jnp.zeros((wide - tenors, flows.shape[1]), f32)], axis=0
+        )
+    held = jnp.concatenate(onehot(bfund_ref[...], split_row(hold_ref[...]), wide), axis=0)
+    quads = dot_cols(held, jnp.concatenate(split(flows), axis=0))
+    weights = (quads[:funds, :wide] + quads[wide : wide + funds, wide:]) + (
+        quads[:funds, wide:] + quads[wide : wide + funds, :wide]
+    )
 
     def put(values, first):
         row = first
@@ -275,7 +275,9 @@
     out_ref,
     table,
     assets_buf,
-    gathered,
+    credited_buf,
+    gathered_even,
+    gathered_odd,
     market_sum,
     staged,
     out_sems,
@@ -335,7 +337,7 @@
                 liab = liab * jnp.exp2(growth)
             ratio = jnp.where(lane < funds, assets_buf[span, :] / liab, 1.0)
             credited = share * jnp.log(ratio)
-            cred_ref[t, :, first : first + tile] = credited.T[:funds]
+            credited_buf[span, :] = credited
             market = market_ref[span, :]
             scaled = (market - credited) * (log2_e / 12.0)
             high, low = split(scaled)
@@ -357,32 +359,43 @@
         cols = pl.ds(pl.multiple_of(idx * block, block), block)
         return pltpu.make_async_copy(staged.at[idx], out_ref.at[:, cols], out_sems.at[idx])
 
-    def fetch(idx, slot):
+    def fetch(idx, gathered):
         cols = pl.ds(pl.multiple_of(idx * block, block), block)
         hot = hot_ref[:, cols]
-        gathered[slot] = dot(table[...], jnp.concatenate([hot, hot], axis=0))
-
-    def settle(idx, slot):
+        gathered[...] = dot(table[...], jnp.concatenate([hot, hot], axis=0))
+
+    def settle(idx, gathered):
         cols = pl.ds(pl.multiple_of(idx * block, block), block)
         first_row = rows[0:1, cols]
         sens_row = rows[1:2, cols]
         for first in range(0, scen, tile):
             acc = first_row + jnp.tile(market_sum[first : first + tile, :], (1, block // lanes))
             for t in range(months):
-                spread = gathered[slot, t * scen + first : t * scen + first + tile, :]
+                spread = gathered[t * scen + first : t * scen + first + tile, :]
                 acc = acc + (rows[2 + t : 3 + t, cols] * jnp.exp2(sens_row * spread) - spread)
             staged[idx, first : first + tile, :] = jnp.exp2(acc)
         out_copy(idx).start()
 
+    def turn(t):
+        span = pl.ds(pl.multiple_of(t * scen, scen), scen)
+        cred_ref[t] = credited_buf[span, :].T[:funds]
+
     blocks = policies // block
-    fetch(0, 0)
-
-    @pl.loop(0, blocks, step=2)
-    def _(idx):
-        fetch(idx + 1, 1)
-        settle(idx, 0)
-        fetch(jnp.minimum(idx + 2, blocks - 1), 0)
-        settle(idx + 1, 1)
+    fetch(0, gathered_even)
+    inside = blocks // 2 >= months
+    if not inside:
+        for t in range(months):
+            turn(t)
+
+    @pl.loop(0, blocks // 2)
+    def _(pair):
+        idx = 2 * pair
+        fetch(idx + 1, gathered_odd)
+        settle(idx, gathered_even)
+        fetch(jnp.minimum(idx + 2, blocks - 1), gathered_even)
+        settle(idx + 1, gathered_odd)
+        if inside:
+            turn(jnp.minimum(pair, months - 1))
 
     @pl.loop(0, blocks)
     def _(idx):
@@ -485,7 +498,9 @@
         scratch_shapes=[
             pltpu.VMEM((months * scen, 2 * wide), bf16),
             pltpu.VMEM((months * scen, wide), f32),
-            pltpu.VMEM((2, months * scen, block), f32),
+            pltpu.VMEM((months * scen, wide), f32),
+            pltpu.VMEM((months * scen, block), f32),
+            pltpu.VMEM((months * scen, block), f32),
             pltpu.VMEM((scen, lanes), f32),
             pltpu.VMEM((policies // block, scen, block), f32),
             pltpu.SemaphoreType.DMA((policies // block,)),

time: 19 us -> 18.7 us (0.984)
  Pallas kernels: 18.2 us -> 17.9 us
    pallas_call x1, Pallas kernels: 5.04 us -> 4.76 us  [local(): pl.pallas_call(functools.partial(project_kernel, kinds, funds, block), ou...]
where the time goes in v3:
time: 18.7 us; the launch traced here: 18.6 us
  Pallas kernels  17.9 us (96%)
  between operations  0.64 us (3%)
    pallas_call x1, Pallas kernels, local(): pl.pallas_call(functools.partial(gather_kernel, group, kinds, funds), out...  13.2 us
    pallas_call x1, Pallas kernels, local(): pl.pallas_call(functools.partial(project_kernel, kinds, funds, block), ou...  4.76 us

profile of v3, /device:TPU:0, one launch (start us, length us, event | category | flops | bytes accessed | tf_op | source)
XLA Modules:
  0.0 18.6 jit_solution(14161230158733355452)
XLA Ops:
  0.6 13.2 %fund_sums.1 = (f32[144,128]{1,0:T(8,128)S(1)}, bf16[128,4096]{1,0:T(8,128)(2,1)S(1)}, f32[8,4096]{1,0:T(8,128)S(1)}, bf16[384,256]{1,0:T(8,128)(2,1)S(1)}, f32[...) custom-call(s32[1,2048]{1,0:T(1,128)} %bitcast.15, f32[1,2048]{1,0:T(1,128)} %bitcast.16, ...), custom_call_target="tpu_custom_call" | custom-call | tf_op jit(solution)/shard_map/fund_sums/pallas_call | solution.py:458
  13.8 4.8 %project.1 = (f32[3,120,128]{2,1,0:T(8,128)}, f32[128,4096]{1,0:T(8,128)}) custom-call(f32[144,128]{1,0:T(8,128)S(1)} %get-tuple-element.9.sums_ref, bf16[128,4096]{1,0:T(8,128)(2,1)S(1)} %get-tuple-element.10.hot_ref, f32[8,4096]{1,0:T(8,128)S(1)} %get-tuple-element.11.rows, bf16[384,256]{1,0:T(8,128)(2,1)S(1)} %get-tuple-element.12.disc_ref, ...), custom_call_target="tpu_custom_call" | custom-call | tf_op jit(solution)/shard_map/project/pallas_call | solution.py:490

commit v4 on v3

--- a/solution.py
+++ b/solution.py
@@ -31,9 +31,9 @@
     return lax.dot_general(left, right, contract_cols, preferred_element_type=f32)
 
 
-def onehot(ids_row, values, row_count):
+def onehot(ids_row, values, row_count, id_limit):
     shape = (16, ids_row.shape[1])
-    kind = bf16 if row_count <= 256 else f32
+    kind = bf16 if max(row_count, id_limit) <= 256 else f32
     ids = jnp.broadcast_to(ids_row.astype(f32), shape).astype(kind)
     rows = lax.broadcasted_iota(jnp.int32, shape, 0).astype(f32)
     values = [jnp.broadcast_to(v, shape).astype(bf16) for v in values]
@@ -85,15 +85,17 @@
     rates_ref,
     in_sems,
     part_buf,
+    core_buf,
     recv_buf,
     sum_buf,
-    send_a,
-    recv_a,
-    send_b,
-    recv_b,
+    core_sems,
+    pol_sems,
+    slot_sems,
 ):
-    pol_devs, fund_devs = group
-    n = pol_devs * fund_devs
+    pol_devs, scen_devs, fund_devs = group
+    at_pol, at_scen, at_fund = (lax.axis_index(name) for name in ("pol", "scen", "fund"))
+    slots = scen_devs * fund_devs
+    slot = at_scen * fund_devs + at_fund
     pairs = (
         (bfund_hbm, bfund_ref),
         (hold_hbm, hold_ref),
@@ -114,34 +116,47 @@
     ]
     for load in loads:
         load.start()
-    me = lax.axis_index("pol") * fund_devs + lax.axis_index("fund")
-
-    def peer_of(step):
-        peer = lax.rem(me + step, n)
-        return peer, {"pol": peer // fund_devs, "fund": lax.rem(peer, fund_devs)}
+
+    def pol_peer(step):
+        peer = lax.rem(at_pol + step, pol_devs)
+        return peer, {"pol": peer}
+
+    def fund_peer(step):
+        peer = lax.rem(at_fund + step, fund_devs)
+        return peer, {"fund": peer}
+
+    def slot_peer(step):
+        peer = lax.rem(slot + step, slots)
+        return peer, {"scen": peer // fund_devs, "fund": lax.rem(peer, fund_devs)}
 
     barrier = pltpu.get_barrier_semaphore()
-    for step in range(1, n):
+    greeted = [pol_peer(step)[1] for step in range(1, pol_devs)]
+    greeted += [slot_peer(step)[1] for step in range(1, slots)]
+    for where in greeted:
         pl.semaphore_signal(
-            barrier, inc=1, device_id=peer_of(step)[1], device_id_type=pl.DeviceIdType.MESH
+            barrier, inc=1, device_id=where, device_id_type=pl.DeviceIdType.MESH
         )
 
     months, tenors, scen = rates_ref.shape
     wide = part_buf.shape[2]
     chunk = part_buf.shape[1]
     part_buf[...] = jnp.zeros_like(part_buf)
+    fund_rows = -(-funds // scen_devs)
+    class_rows = -(-(months * kinds) // scen_devs)
 
     for load in loads[3:8]:
         load.wait()
     worth = count_ref[...] * value_ref[...]
     late = jnp.clip(dur_ref[...] - (surrender_end - (months - 1)), 0, months - 1)
     kind = late * kinds + prod_ref[...]
-    classed = onehot(kind, split_row(worth), round_up(months * kinds, 16))
-    (pol_hot,) = onehot(pfund_ref[...], [jnp.ones(worth.shape, f32)], wide)
+    classed = onehot(
+        kind - at_scen * class_rows, split_row(worth), round_up(class_rows, 16), months * kinds
+    )
+    (pol_hot,) = onehot(pfund_ref[...], [jnp.ones(worth.shape, f32)], wide, funds)
     hot_ref[...] = pol_hot
     sides = dot_cols(jnp.concatenate(classed, axis=0), pol_hot)
     half = sides.shape[0] // 2
-    classes = (sides[:half] + sides[half:])[: months * kinds]
+    classes = (sides[:half] + sides[half:])[:class_rows]
 
     for load in loads[:3]:
         load.wait()
@@ -150,62 +165,63 @@
         flows = jnp.concatenate(
             [flows, jnp.zeros((wide - tenors, flows.shape[1]), f32)], axis=0
         )
-    held = jnp.concatenate(onehot(bfund_ref[...], split_row(hold_ref[...]), wide), axis=0)
+    held_rows = round_up(fund_rows, 16)
+    held = onehot(
+        bfund_ref[...] - at_scen * fund_rows, split_row(hold_ref[...]), held_rows, funds
+    )
+    held = jnp.concatenate(held, axis=0)
     quads = dot_cols(held, jnp.concatenate(split(flows), axis=0))
-    weights = (quads[:funds, :wide] + quads[wide : wide + funds, wide:]) + (
-        quads[:funds, wide:] + quads[wide : wide + funds, :wide]
-    )
+    upper, lower = quads[:fund_rows], quads[held_rows : held_rows + fund_rows]
+    weights = (upper[:, :wide] + lower[:, wide:]) + (upper[:, wide:] + lower[:, :wide])
 
     def put(values, first):
         row = first
         while row < first + values.shape[0]:
-            slot, inner = row // chunk, row % chunk
+            core, inner = row // chunk, row % chunk
             size = min(chunk - inner, first + values.shape[0] - row)
-            part_buf[slot, inner : inner + size, : values.shape[1]] = values[
+            part_buf[core, inner : inner + size, : values.shape[1]] = values[
                 row - first : row - first + size
             ]
             row += size
 
     put(weights, 0)
-    put(classes, funds)
-
-    pl.semaphore_wait(barrier, n - 1)
-
-    def scatter(step):
-        peer, where = peer_of(step)
+    put(classes, fund_rows)
+
+    pl.semaphore_wait(barrier, len(greeted))
+
+    def send(src, dst, sems, mine, to):
+        peer, where = to
         return pltpu.make_async_remote_copy(
-            src_ref=part_buf.at[peer],
-            dst_ref=recv_buf.at[me],
-            send_sem=send_a.at[peer],
-            recv_sem=recv_a.at[me],
+            src_ref=src,
+            dst_ref=dst,
+            send_sem=sems.at[0, peer],
+            recv_sem=sems.at[1, mine],
             device_id=where,
             device_id_type=pl.DeviceIdType.MESH,
         )
 
-    def spread(step):
-        peer, where = peer_of(step)
-        return pltpu.make_async_remote_copy(
-            src_ref=sum_buf.at[me],
-            dst_ref=sum_buf.at[me],
-            send_sem=send_b.at[peer],
-            recv_sem=recv_b.at[me],
-            device_id=where,
-            device_id_type=pl.DeviceIdType.MESH,
-        )
-
-    def arrival(buf, sems, step):
-        peer, where = peer_of(step)
-        return pltpu.make_async_remote_copy(
-            src_ref=buf.at[peer],
-            dst_ref=buf.at[peer],
-            send_sem=send_a.at[peer],
-            recv_sem=sems.at[peer],
-            device_id=where,
-            device_id_type=pl.DeviceIdType.MESH,
-        )
-
-    for step in range(1, n):
-        scatter(step).start()
+    def arrive(buf, sems, to):
+        peer = to[0]
+        send(buf.at[peer], buf.at[peer], sems, peer, to).wait_recv()
+
+    swaps = [
+        send(part_buf.at[fund_peer(i)[0]], core_buf.at[at_fund], core_sems, at_fund, fund_peer(i))
+        for i in range(1, fund_devs)
+    ]
+    for copy in swaps:
+        copy.start()
+    half_sum = part_buf[at_fund]
+    for i in range(1, fund_devs):
+        arrive(core_buf, core_sems, fund_peer(i))
+        half_sum = half_sum + core_buf[fund_peer(i)[0]]
+    recv_buf[at_pol] = half_sum
+
+    parts = [
+        send(recv_buf.at[at_pol], recv_buf.at[at_pol], pol_sems, at_pol, pol_peer(i))
+        for i in range(1, pol_devs)
+    ]
+    for copy in parts:
+        copy.start()
 
     for load in loads[8:]:
         load.wait()
@@ -231,13 +247,19 @@
             dur_ref[...] + t >= surrender_end, -2.0 * log2_e, -log2_e
         )
 
-    total = part_buf[me]
-    for step in range(1, n):
-        arrival(recv_buf, recv_a, step).wait_recv()
-        total = total + recv_buf[peer_of(step)[0]]
-    sum_buf[me] = total
-    for step in range(1, n):
-        spread(step).start()
+    for i in range(1, pol_devs):
+        arrive(recv_buf, pol_sems, pol_peer(i))
+    total = recv_buf[0]
+    for i in range(1, pol_devs):
+        total = total + recv_buf[i]
+    sum_buf[slot] = total
+
+    wholes = [
+        send(sum_buf.at[slot], sum_buf.at[slot], slot_sems, slot, slot_peer(i))
+        for i in range(1, slots)
+    ]
+    for copy in wholes:
+        copy.start()
 
     tenor_years = (
         lax.broadcasted_iota(jnp.int32, (1, tenors), 1).astype(f32) + 1.0
@@ -251,16 +273,21 @@
         disc_ref[span, wide : wide + tenors] = disc_l
         market_ref[span, :] = jnp.broadcast_to(rates[:, tenors - 1 : tenors], (scen, wide))
 
-    for step in range(1, n):
-        arrival(sum_buf, recv_b, step).wait_recv()
-    for slot in range(n):
-        out_ref[slot * chunk : (slot + 1) * chunk, :] = sum_buf[slot]
-    for step in range(1, n):
-        scatter(step).wait_send()
-        spread(step).wait_send()
+    for i in range(1, slots):
+        arrive(sum_buf, slot_sems, slot_peer(i))
+    for column in range(scen_devs):
+        block = jnp.concatenate(
+            [sum_buf[column * fund_devs + core] for core in range(fund_devs)], axis=0
+        )
+        out_ref[column * fund_rows : (column + 1) * fund_rows, :] = block[:fund_rows]
+        first = scen_devs * fund_rows + column * class_rows
+        out_ref[first : first + class_rows, :] = block[fund_rows : fund_rows + class_rows]
+    for copy in swaps + parts + wholes:
+        copy.wait_send()
 
 
 def project_kernel(
+    class_at,
     kinds,
     funds,
     block,
@@ -305,7 +332,7 @@
         [kind_ref[i * kinds + k : i * kinds + k + 1, :] for k in range(kinds)] for i in range(3)
     )
     start = [
-        [[sums_ref[funds + u * kinds + k : funds + u * kinds + k + 1, :] for k in range(kinds)]
+        [[sums_ref[class_at + u * kinds + k : class_at + u * kinds + k + 1, :] for k in range(kinds)]
          for u in range(months)]
     ]
     for t in range(1, months):
@@ -422,9 +449,11 @@
     months, tenors, scen = scen_rates.shape
     kinds = lapse_base.shape[0]
     policies = count_init.shape[0]
-    n = group[0] * group[1]
+    pol_devs, scen_devs, fund_devs = group
+    fund_rows = -(-funds // scen_devs)
+    class_rows = -(-(months * kinds) // scen_devs)
     wide = round_up(max(funds, tenors), lanes)
-    chunk = -(-(funds + months * kinds) // n)
+    chunk = -(-(fund_rows + class_rows) // fund_devs)
     vmem = pl.BlockSpec(memory_space=pltpu.VMEM)
     count_row, value_row, dur_row, prod_row, pfund_row, bfund_row, hold_row = (
         x[None, :]
@@ -458,7 +487,7 @@
     carried = pl.pallas_call(
         functools.partial(gather_kernel, group, kinds, funds),
         out_shape=(
-            jax.ShapeDtypeStruct((n * chunk, wide), f32),
+            jax.ShapeDtypeStruct((scen_devs * (fund_rows + class_rows), wide), f32),
             jax.ShapeDtypeStruct((wide, policies), bf16),
             jax.ShapeDtypeStruct((round_up(2 + months, 8), policies), f32),
             jax.ShapeDtypeStruct((months * scen, 2 * wide), bf16),
@@ -473,13 +502,13 @@
             *(pltpu.SMEM(x.shape, x.dtype) for x in sources[8:11]),
             pltpu.VMEM(scen_rates.shape, f32),
             pltpu.SemaphoreType.DMA((len(sources),)),
-            pltpu.VMEM((n, chunk, wide), f32),
-            pltpu.VMEM((n, chunk, wide), f32),
-            pltpu.VMEM((n, chunk, wide), f32),
-            pltpu.SemaphoreType.DMA((n,)),
-            pltpu.SemaphoreType.DMA((n,)),
-            pltpu.SemaphoreType.DMA((n,)),
-            pltpu.SemaphoreType.DMA((n,)),
+            pltpu.VMEM((fund_devs, chunk, wide), f32),
+            pltpu.VMEM((fund_devs, chunk, wide), f32),
+            pltpu.VMEM((pol_devs, chunk, wide), f32),
+            pltpu.VMEM((scen_devs * fund_devs, chunk, wide), f32),
+            pltpu.SemaphoreType.DMA((2, fund_devs)),
+            pltpu.SemaphoreType.DMA((2, pol_devs)),
+            pltpu.SemaphoreType.DMA((2, scen_devs * fund_devs)),
         ],
         compiler_params=pltpu.CompilerParams(
             collective_id=0, has_side_effects=True, vmem_limit_bytes=few
@@ -488,7 +517,7 @@
     )(*(pltpu.with_memory_space_constraint(x, pltpu.HBM) for x in sources))
     block = policies // (2 * max(1, policies // 512))
     return pl.pallas_call(
-        functools.partial(project_kernel, kinds, funds, block),
+        functools.partial(project_kernel, scen_devs * fund_rows, kinds, funds, block),
         out_shape=(
             jax.ShapeDtypeStruct((months, funds, scen), f32),
             jax.ShapeDtypeStruct((scen, policies), f32),
@@ -527,7 +556,7 @@
         P(None, None, ("parts", "scen")),
     )
     out_specs = (P(None, None, ("parts", "scen")), P(("parts", "scen"), ("pol", "fund")))
-    group = (mesh.shape["pol"], mesh.shape["fund"])
+    group = tuple(mesh.shape[name] for name in ("pol", "scen", "fund"))
     return jax.shard_map(
         functools.partial(local, group),
         mesh=mesh,

time: 18.7 us -> 19.1 us (1.021)
  Pallas kernels: 17.9 us -> 18.3 us
    pallas_call x1, Pallas kernels: 13.2 us -> 13.6 us  [local(): pl.pallas_call(functools.partial(gather_kernel, group, kinds, funds), out...]
where the time goes in v4:
time: 19.1 us; the launch traced here: 19 us
  Pallas kernels  18.3 us (96%)
  between operations  0.64 us (3%)
    pallas_call x1, Pallas kernels, local(): pl.pallas_call(functools.partial(gather_kernel, group, kinds, funds), out...  13.6 us
    pallas_call x1, Pallas kernels, local(): pl.pallas_call(functools.partial(project_kernel, scen_devs * fund_rows, k...  4.76 us

profile of v4, /device:TPU:0, one launch (start us, length us, event | category | flops | bytes accessed | tf_op | source)
XLA Modules:
  0.0 19.0 jit_solution(16991737049359371738)
XLA Ops:
  0.6 13.6 %fund_sums.1 = (f32[144,128]{1,0:T(8,128)S(1)}, bf16[128,4096]{1,0:T(8,128)(2,1)S(1)}, f32[8,4096]{1,0:T(8,128)S(1)}, bf16[384,256]{1,0:T(8,128)(2,1)S(1)}, f32[...) custom-call(s32[1,2048]{1,0:T(1,128)} %bitcast.15, f32[1,2048]{1,0:T(1,128)} %bitcast.16, ...), custom_call_target="tpu_custom_call" | custom-call | tf_op jit(solution)/shard_map/fund_sums/pallas_call | solution.py:487
  14.2 4.8 %project.1 = (f32[3,120,128]{2,1,0:T(8,128)}, f32[128,4096]{1,0:T(8,128)}) custom-call(f32[144,128]{1,0:T(8,128)S(1)} %get-tuple-element.9.sums_ref, bf16[128,4096]{1,0:T(8,128)(2,1)S(1)} %get-tuple-element.10.hot_ref, f32[8,4096]{1,0:T(8,128)S(1)} %get-tuple-element.11.rows, bf16[384,256]{1,0:T(8,128)(2,1)S(1)} %get-tuple-element.12.disc_ref, ...), custom_call_target="tpu_custom_call" | custom-call | tf_op jit(solution)/shard_map/project/pallas_call | solution.py:519
